TPU v7x, 32 devices: a whole 2x2x4 slice. The times are simulated.
32 devices in a mesh: cuts: 4 (over z), tile: 8 (over y, x, core).
Axes of the slice: x: 2, y: 2, z: 4, core: 2. Of those that a mesh axis runs over, the one named last changes fastest.
Arguments:
- start_states: float32 [4, 3, 128, 2048], P('cuts', None, 'tile'), may hold values from -6 to 6
Outputs:
- next_states: float32 [4, 3, 128, 2048], P('cuts', None, 'tile')
All inputs are finite; a program needn't handle non-finite values.
Results may differ from a plain program's by a relative error of at most 0.0001.
Values sent between devices are 32-bit elements; how exact they have to be, the bound alone decides.
A program may use at most 128 MiB of HBM per device.

v0:
```python
import jax
import jax.numpy as jnp
from jax import lax
from jax.sharding import PartitionSpec as P

STEPS = 3


FINE_SPACING = 0.05
COARSE_SPACING = 0.1
FINE_STEP = 0.015
COARSE_STEP = 0.045


def extended(shard, sides, width):
    for axis, dim in sides:
        size, length = (lax.axis_size(axis), shard.shape[dim])
        up = [(i, (i + 1) % size) for i in range(size - 1)]
        down = [(j, i) for i, j in up]
        last = lax.slice_in_dim(shard, length - width, length, axis=dim)
        first = lax.slice_in_dim(shard, 0, width, axis=dim)
        before = lax.ppermute(last, axis, up)
        after = lax.ppermute(first, axis, down)
        shard = jnp.concatenate([before, shard, after], axis=dim)
    return shard


def passed_along(block, axis, distance):
    devices = range(lax.axis_size(axis))
    route = [(i - distance, i) for i in devices if i - distance in devices]
    return lax.ppermute(block, axis, route)


def depth_profile(columns, stride, length):
    centers = (jnp.arange(columns).astype(jnp.float32) + 0.5) * stride
    return 0.9 + 0.3 * jnp.sin(6.0 * jnp.pi * centers / length)


def along_x(values, spacing):
    padded = jnp.pad(values, [(0, 0)] * (values.ndim - 1) + [(1, 1)])
    return (padded[..., 2:] - padded[..., :-2]) / (2.0 * spacing)


def along_y(values, spacing):
    padded = jnp.pad(values, [(0, 0)] * (values.ndim - 2) + [(1, 1), (0, 0)])
    return (padded[..., 2:, :] - padded[..., :-2, :]) / (2.0 * spacing)


def second_y(values):
    padded = jnp.pad(values, [(0, 0)] * (values.ndim - 2) + [(1, 1), (0, 0)])
    return padded[..., 2:, :] - 2.0 * values + padded[..., :-2, :]


def reduce_lines(lower, middle, upper, rhs):
    length = rhs.shape[-1]
    if length == 1:
        return rhs / middle
    leading = rhs.shape[:-1]
    pairs = rhs.reshape(leading + (length // 2, 2))
    rhs_even = pairs[..., 0]
    rhs_odd = pairs[..., 1]
    lower_even = lower[0::2]
    lower_odd = lower[1::2]
    middle_even = middle[0::2]
    middle_odd = middle[1::2]
    upper_even = upper[0::2]
    upper_odd = upper[1::2]
    one_more = jnp.ones((1,), jnp.float32)
    no_more = jnp.zeros((1,), jnp.float32)
    middle_after = jnp.concatenate([middle_even[1:], one_more])
    lower_after = jnp.concatenate([lower_even[1:], no_more])
    upper_after = jnp.concatenate([upper_even[1:], no_more])
    rhs_after = jnp.concatenate(
        [rhs_even[..., 1:], jnp.zeros(leading + (1,), jnp.float32)], axis=-1
    )
    alpha = -lower_odd / middle_even
    gamma = -upper_odd / middle_after
    new_lower = alpha * lower_even
    new_middle = middle_odd + alpha * upper_even + gamma * lower_after
    new_upper = gamma * upper_after
    new_rhs = rhs_odd + alpha * rhs_even + gamma * rhs_after
    solved_odd = reduce_lines(new_lower, new_middle, new_upper, new_rhs)
    odd_before = jnp.concatenate(
        [jnp.zeros(leading + (1,), jnp.float32), solved_odd[..., :-1]], axis=-1
    )
    solved_even = (rhs_even - lower_even * odd_before - upper_even * solved_odd) / middle_even
    return jnp.stack([solved_even, solved_odd], axis=-1).reshape(leading + (length,))


def solve_lines(forcing, seabed, spacing):
    columns = forcing.shape[-1]
    coupling = seabed * seabed / (3.0 * spacing * spacing)
    below_diag = (-coupling).at[0].set(0.0)
    above_diag = (-coupling).at[columns - 1].set(0.0)
    middle = 1.0 + 2.0 * coupling
    solved = reduce_lines(below_diag, middle, above_diag, forcing)
    return solved


def wave_step(fields, seabed, spacing, time_step, inside):
    height = fields[0]
    flux_x = fields[1]
    flux_y = fields[2]
    height_new = (
        height - time_step * (along_x(flux_x, spacing) + along_y(flux_y, spacing))
    ) * inside
    forcing = jnp.stack(
        [
            flux_x - time_step * seabed * along_x(height_new, spacing),
            flux_y - time_step * seabed * along_y(height_new, spacing),
        ],
        axis=0,
    )
    trial_flux = solve_lines(forcing, seabed, spacing) * inside
    dispersion = seabed * seabed / 3.0
    weight = dispersion / (spacing * spacing + 4.0 * dispersion)
    fluxes_new = (trial_flux + weight * second_y(trial_flux - fields[1:])) * inside
    return jnp.concatenate([height_new[None], fluxes_new], axis=0)


def restrict(fields):
    planes = fields.shape[0]
    row_count = fields.shape[1]
    columns = fields.shape[2]
    blocks = fields.reshape(planes, row_count // 2, 2, columns // 2, 2)
    return 0.25 * jnp.sum(blocks, axis=(2, 4))


def prolong(coarse):
    return jnp.repeat(jnp.repeat(coarse, 2, axis=1), 2, axis=2)


def per_device(start_states):
    fields = start_states[0]
    row_count = fields.shape[1]
    columns = fields.shape[2]
    tile_count = lax.axis_size("tile")
    first_row = lax.axis_index("tile") * row_count
    total_rows = row_count * tile_count
    fine_depth = depth_profile(columns, 1.0, columns)
    coarse_depth = depth_profile(columns // 2, 2.0, columns)

    def row_mask(local_rows, margin, factor):
        offsets = (
            jnp.arange(local_rows + 2 * margin, dtype=jnp.int32) - margin + first_row // factor
        )
        return ((offsets >= 0) & (offsets < total_rows // factor)).astype(jnp.float32)[:, None]

    inside = row_mask(row_count, 3, 1)
    fine_end = fields
    for substep in range(STEPS):
        widened = extended(fine_end, (("tile", 1),), 3)
        fine_end = wave_step(widened, fine_depth, FINE_SPACING, FINE_STEP, inside)[
            :, 3 : 3 + row_count
        ]
    coarse_rows = row_count // 2
    coarse_inside = row_mask(coarse_rows, 3, 2)

    def coarse_step(values):
        widened_coarse = extended(values, (("tile", 1),), 3)
        return wave_step(widened_coarse, coarse_depth, COARSE_SPACING, COARSE_STEP, coarse_inside)[
            :, 3 : 3 + coarse_rows
        ]

    restricted_start = restrict(fields)
    restricted_end = restrict(fine_end)

    def propagate(current):
        return coarse_step(current - restricted_start)

    cut_index = lax.axis_index("cuts")
    slices = lax.axis_size("cuts")
    current = restricted_start
    for link_step in range(slices - 1):
        arrived = passed_along(propagate(current) + restricted_end, "cuts", 1)
        current = jnp.where(cut_index == link_step + 1, arrived, current)
    return (prolong(propagate(current)) + fine_end)[None]


def solution(mesh):
    in_specs = (P("cuts", None, "tile", None),)
    out_specs = P("cuts", None, "tile", None)
    return jax.shard_map(
        per_device, mesh=mesh, in_specs=in_specs, out_specs=out_specs, check_vma=False
    )
```

profile of v0, /device:TPU:27, one launch (start us, length us, event | category | flops | bytes accessed | tf_op | source)
XLA Modules:
  0.0 417.5 jit_solution(979300366475339465)
XLA Ops:
  1.1 3.7 collective-permute-start.2
  4.7 1.9 collective-permute-start.3
  6.7 28.5 %reshape_squeeze.3 = f32[3,8,2,1024,2]{4,3,2,1,0:T(8,128)} reshape(f32[1,3,16,2048]{3,2,1,0:T(8,128)} %param.29) | data formatting | bytes 786432 | tf_op jit(solution)/shard_map/reshape;squeeze | solution.py:125
  35.1 10.2 %reduce_sum.18 = f32[3,8,1024]{2,1,0:T(8,128)S(1)} reduce(f32[3,8,2,1024,2]{4,3,2,1,0:T(8,128)} %reshape_squeeze.3, f32[]{:T(128)} %constant.342.clone.1), dimensions={2,4}, to_apply=%region_0.1 | reduce | flops 73728 | bytes 491524 | tf_op jit(solution)/shard_map/reduce_sum | solution.py:126
  45.4 4.5 %collective-permute-start = (f32[3,3,1024]{2,1,0:T(4,128)S(1)}, f32[3,3,1024]{2,1,0:T(4,128)S(1)}, u32[]{:S(2)}, u32[]{:S(2)}) collective-permute-start(f32[3,3,1024]{2,1,0:T(4,128)S(1)} %get-tuple-element.318), channel_id=1, source_target_pairs={{0,1},{1,2},{2,3},{3,4},{4,5},{5,6},{6,7},{8,9},{9,10},{10,11},{11... | collective-permute-start | bytes 110600 | tf_op jit(solution)/shard_map/ppermute | solution.py:22
  50.0 2.4 collective-permute-start.1
  131.1 1.2 slice.2596
  132.9 1.2 slice.2591
  134.1 1.3 fusion.121
  135.4 1.3 fusion.123
  138.7 1.2 slice.2432
  139.9 1.3 slice.2442
  143.1 1.4 fusion.118
  144.5 1.3 fusion.120
  172.5 1.4 copy.1594
  173.8 1.8 fusion.7
  176.6 2.1 pad_maximum_fusion.4
  183.0 1.2 subtract_divide_fusion.5
  191.2 1.6 copy.1362
  192.9 2.0 copy.1606
  194.9 1.8 multiply_subtract_fusion.2
  196.7 2.8 add_multiply_fusion.2
  199.5 2.2 copy.1365
  202.1 4.5 %collective-permute-start.4 = (f32[3,3,2048]{2,1,0:T(4,128)S(1)}, f32[3,3,2048]{2,1,0:T(4,128)S(1)}, u32[]{:S(2)}, u32[]{:S(2)}) collective-permute-start(f32[3,3,2048]{2,1,0:T(4,128)S(1)} %get-tuple-element.247), channel_id=1, source_target_pairs={{0,1},{1,2},{2,3},{3,4},{4,5},{5,6},{6,7},{8,9},{9,10},{10,11},{11... | collective-permute-start | bytes 221192 | tf_op jit(solution)/shard_map/ppermute | solution.py:22
  206.6 2.3 collective-permute-start.5
  209.0 4.4 %collective-permute-done.5 = f32[3,3,2048]{2,1,0:T(4,128)S(1)} collective-permute-done((f32[3,3,2048]{2,1,0:T(4,128)S(1)}, f32[3,3,2048]{2,1,0:T(4,128)S(1)}, u32[]{:S(2)}, u32[]{:S(2)}) %collective-permute-start.5) | collective-permute-done | bytes 73760 | tf_op jit(solution)/shard_map/ppermute | solution.py:23
  215.1 1.4 copy.1607
  216.5 1.8 fusion.6
  224.3 1.2 subtract_divide_fusion.4
  232.6 1.6 copy.1405
  234.2 2.0 copy.1626
  236.2 1.8 multiply_subtract_fusion.1
  238.1 2.9 add_multiply_fusion.1
  241.0 2.2 copy.1408
  243.6 1.9 collective-permute-start.6
  245.6 2.4 collective-permute-start.7
  248.0 4.4 %collective-permute-done.7 = f32[3,3,2048]{2,1,0:T(4,128)S(1)} collective-permute-done((f32[3,3,2048]{2,1,0:T(4,128)S(1)}, f32[3,3,2048]{2,1,0:T(4,128)S(1)}, u32[]{:S(2)}, u32[]{:S(2)}) %collective-permute-start.7) | collective-permute-done | bytes 73760 | tf_op jit(solution)/shard_map/ppermute | solution.py:23
  254.0 1.4 copy.1627
  255.4 1.8 fusion.5
  271.5 1.6 copy.1452
  273.2 2.0 copy.1638
  275.2 1.8 multiply_subtract_fusion
  277.0 1.8 add_multiply_fusion
  278.8 1.3 copy-done
  280.2 2.6 pad_maximum_fusion
  282.7 2.3 copy.1454
  285.1 27.6 %reshape.1034 = f32[3,8,2,1024,2]{4,3,2,1,0:T(8,128)} reshape(f32[3,16,2048]{2,1,0:T(8,128)S(1)} %copy.1454) | data formatting | bytes 786432 | tf_op jit(solution)/shard_map/reshape | solution.py:125
  312.7 10.2 %reduce_sum.19 = f32[3,8,1024]{2,1,0:T(8,128)S(1)} reduce(f32[3,8,2,1024,2]{4,3,2,1,0:T(8,128)} %reshape.1034, f32[]{:T(128)} %constant.342.clone.1), dimensions={2,4}, to_apply=%region_1.2 | reduce | flops 73728 | bytes 491524 | tf_op jit(solution)/shard_map/reduce_sum | solution.py:126
  323.0 1.3 collective-permute-start.8
  324.3 4.1 collective-permute-done.8
  328.4 1.9 collective-permute-start.10
  330.4 4.5 %collective-permute-start.9 = (f32[3,3,1024]{2,1,0:T(4,128)S(1)}, f32[3,3,1024]{2,1,0:T(4,128)S(1)}, u32[]{:S(2)}, u32[]{:S(2)}) collective-permute-start(f32[3,3,1024]{2,1,0:T(4,128)S(1)} %get-tuple-element.316), channel_id=1, source_target_pairs={{0,1},{1,2},{2,3},{3,4},{4,5},{5,6},{6,7},{8,9},{9,10},{10,11},{11... | collective-permute-start | bytes 110600 | tf_op jit(solution)/shard_map/ppermute | solution.py:22
  349.9 1.3 collective-permute-start.11
  351.2 4.9 %collective-permute-done.11 = f32[3,8,1024]{2,1,0:T(8,128)S(1)} collective-permute-done((f32[3,8,1024]{2,1,0:T(8,128)S(1)}, f32[3,8,1024]{2,1,0:T(8,128)S(1)}, u32[]{:S(2)}, u32[]{:S(2)}) %collective-permute-start.11) | collective-permute-done | bytes 98336 | tf_op jit(solution)/shard_map/ppermute | solution.py:31
  356.2 5.4 %collective-permute-start.12 = (f32[3,3,1024]{2,1,0:T(4,128)S(1)}, f32[3,3,1024]{2,1,0:T(4,128)S(1)}, u32[]{:S(2)}, u32[]{:S(2)}) collective-permute-start(f32[3,3,1024]{2,1,0:T(4,128)S(1)} %get-tuple-element.314), channel_id=1, source_target_pairs={{0,1},{1,2},{2,3},{3,4},{4,5},{5,6},{6,7},{8,9},{9,10},{10,11},{11... | collective-permute-start | bytes 110600 | tf_op jit(solution)/shard_map/ppermute | solution.py:22
  361.6 2.1 collective-permute-start.13
  363.8 4.2 %collective-permute-done.13 = f32[3,3,1024]{2,1,0:T(4,128)S(1)} collective-permute-done((f32[3,3,1024]{2,1,0:T(4,128)S(1)}, f32[3,3,1024]{2,1,0:T(4,128)S(1)}, u32[]{:S(2)}, u32[]{:S(2)}) %collective-permute-start.13) | collective-permute-done | bytes 36896 | tf_op jit(solution)/shard_map/ppermute | solution.py:23
  381.4 1.3 collective-permute-start.14
  382.7 4.1 collective-permute-done.14
  386.8 3.0 collective-permute-start.15
  389.8 1.9 collective-permute-start.16
  391.8 4.4 %collective-permute-done.16 = f32[3,3,1024]{2,1,0:T(4,128)S(1)} collective-permute-done((f32[3,3,1024]{2,1,0:T(4,128)S(1)}, f32[3,3,1024]{2,1,0:T(4,128)S(1)}, u32[]{:S(2)}, u32[]{:S(2)}) %collective-permute-start.16) | collective-permute-done | bytes 36896 | tf_op jit(solution)/shard_map/ppermute | solution.py:23
  411.8 2.6 add_bitcast_fusion
  414.3 3.0 copy.1573
  (1191 shorter events, 185.7 us)
Async XLA Ops:
  1.1 169.8 %collective-permute-start.2 = (f32[3,3,2048]{2,1,0:T(4,128)S(1)}, f32[3,3,2048]{2,1,0:T(4,128)S(1)}, u32[]{:S(2)}, u32[]{:S(2)}) collective-permute-start(f32[3,3,2048]{2,1,0:T(4,128)S(1)} %get-tuple-element.266), channel_id=1, source_target_pairs={{0,1},{1,2},{2,3},{3,4},{4,5},{5,6},{6,7},{8,9},{9,10},{10,11},{11... | collective-permute-start | bytes 221192 | tf_op jit(solution)/shard_map/ppermute | solution.py:22
  4.7 166.1 %collective-permute-start.3 = (f32[3,3,2048]{2,1,0:T(4,128)S(1)}, f32[3,3,2048]{2,1,0:T(4,128)S(1)}, u32[]{:S(2)}, u32[]{:S(2)}) collective-permute-start(f32[3,3,2048]{2,1,0:T(4,128)S(1)} %get-tuple-element.267), channel_id=1, source_target_pairs={{1,0},{2,1},{3,2},{4,3},{5,4},{6,5},{7,6},{9,8},{10,9},{11,10},{12... | collective-permute-start | bytes 221192 | tf_op jit(solution)/shard_map/ppermute | solution.py:23
  45.4 112.2 %copy-start.5 = (f32[3,8,1024]{2,1,0:T(8,128)}, f32[3,8,1024]{2,1,0:T(8,128)S(1)}, u32[]{:S(2)}) copy-start(f32[3,8,1024]{2,1,0:T(8,128)S(1)} %reduce_sum.18) | copy-start | bytes 294916
  45.4 109.7 %collective-permute-start = (f32[3,3,1024]{2,1,0:T(4,128)S(1)}, f32[3,3,1024]{2,1,0:T(4,128)S(1)}, u32[]{:S(2)}, u32[]{:S(2)}) collective-permute-start(f32[3,3,1024]{2,1,0:T(4,128)S(1)} %get-tuple-element.318), channel_id=1, source_target_pairs={{0,1},{1,2},{2,3},{3,4},{4,5},{5,6},{6,7},{8,9},{9,10},{10,11},{11... | collective-permute-start | bytes 110600 | tf_op jit(solution)/shard_map/ppermute | solution.py:22
  50.0 105.2 %collective-permute-start.1 = (f32[3,3,1024]{2,1,0:T(4,128)S(1)}, f32[3,3,1024]{2,1,0:T(4,128)S(1)}, u32[]{:S(2)}, u32[]{:S(2)}) collective-permute-start(f32[3,3,1024]{2,1,0:T(4,128)S(1)} %get-tuple-element.319), channel_id=1, source_target_pairs={{1,0},{2,1},{3,2},{4,3},{5,4},{6,5},{7,6},{9,8},{10,9},{11,10},{12... | collective-permute-start | bytes 110600 | tf_op jit(solution)/shard_map/ppermute | solution.py:23
  53.9 124.8 %copy-start.23 = (f32[1024]{0:T(1024)}, f32[1024]{0:T(1024)S(1)}, u32[]{:S(2)}) copy-start(f32[1024]{0:T(1024)S(1)} %get-tuple-element.182) | copy-start | bytes 12292
  54.2 135.2 %copy-start.37 = (f32[512]{0:T(512)}, f32[512]{0:T(512)S(1)}, u32[]{:S(2)}) copy-start(f32[512]{0:T(512)S(1)} %slice.2481) | copy-start | bytes 6148
  54.5 124.2 %copy-start.26 = (f32[1024]{0:T(1024)}, f32[1024]{0:T(1024)S(1)}, u32[]{:S(2)}) copy-start(f32[1024]{0:T(1024)S(1)} %get-tuple-element.184) | copy-start | bytes 12292
  54.8 134.6 %copy-start.40 = (f32[512]{0:T(512)}, f32[512]{0:T(512)S(1)}, u32[]{:S(2)}) copy-start(f32[512]{0:T(512)S(1)} %slice.2497) | copy-start | bytes 6148
  55.3 134.1 %copy-start.43 = (f32[512]{0:T(512)}, f32[512]{0:T(512)S(1)}, u32[]{:S(2)}) copy-start(f32[512]{0:T(512)S(1)} %slice.2487) | copy-start | bytes 6148
  55.8 112.4 %copy-start.29 = (f32[512]{0:T(512)}, f32[512]{0:T(512)S(1)}, u32[]{:S(2)}) copy-start(f32[512]{0:T(512)S(1)} %slice.2331) | copy-start | bytes 6148
  56.3 112.0 %copy-start.31 = (f32[512]{0:T(512)}, f32[512]{0:T(512)S(1)}, u32[]{:S(2)}) copy-start(f32[512]{0:T(512)S(1)} %slice.2343) | copy-start | bytes 6148
  56.7 111.5 %copy-start.33 = (f32[512]{0:T(512)}, f32[512]{0:T(512)S(1)}, u32[]{:S(2)}) copy-start(f32[512]{0:T(512)S(1)} %slice.2334) | copy-start | bytes 6148
  57.1 90.5 %copy-start.50 = (f32[512]{0:T(512)}, f32[512]{0:T(512)S(1)}, u32[]{:S(2)}) copy-start(f32[512]{0:T(512)S(1)} %get-tuple-element.178) | copy-start | bytes 6148
  57.3 100.2 %copy-start.68 = (f32[256]{0:T(256)}, f32[256]{0:T(256)S(1)}, u32[]{:S(2)}) copy-start(f32[256]{0:T(256)S(1)} %slice.2493) | copy-start | bytes 3076
  57.7 99.9 %copy-start.54 = (f32[512]{0:T(512)}, f32[512]{0:T(512)S(1)}, u32[]{:S(2)}) copy-start(f32[512]{0:T(512)S(1)} %get-tuple-element.180) | copy-start | bytes 6148
  58.0 99.7 %copy-start.76 = (f32[256]{0:T(256)}, f32[256]{0:T(256)S(1)}, u32[]{:S(2)}) copy-start(f32[256]{0:T(256)S(1)} %slice.2509) | copy-start | bytes 3076
  58.3 99.4 %copy-start.46 = (f32[512]{0:T(512)}, f32[512]{0:T(512)S(1)}, u32[]{:S(2)}) copy-start(f32[512]{0:T(512)S(1)} %get-tuple-element.220) | copy-start | bytes 6148
  58.5 99.2 %copy-start.48 = (f32[512]{0:T(512)}, f32[512]{0:T(512)S(1)}, u32[]{:S(2)}) copy-start(f32[512]{0:T(512)S(1)} %get-tuple-element.222) | copy-start | bytes 6148
  58.8 98.8 %copy-start.72 = (f32[256]{0:T(256)}, f32[256]{0:T(256)S(1)}, u32[]{:S(2)}) copy-start(f32[256]{0:T(256)S(1)} %slice.2499) | copy-start | bytes 3076
  59.2 30.8 %copy-start.84 = (f32[256]{0:T(256)}, f32[256]{0:T(256)S(1)}, u32[]{:S(2)}) copy-start(f32[256]{0:T(256)S(1)} %get-tuple-element.174) | copy-start | bytes 3076
  59.8 28.7 %copy-start.88 = (f32[256]{0:T(256)}, f32[256]{0:T(256)S(1)}, u32[]{:S(2)}) copy-start(f32[256]{0:T(256)S(1)} %get-tuple-element.176) | copy-start | bytes 3076
  62.3 27.1 %copy-start.138 = (f32[64]{0:T(128)}, f32[64]{0:T(128)S(1)}, u32[]{:S(2)}) copy-start(f32[64]{0:T(128)S(1)} %get-tuple-element.166) | copy-start | bytes 772
  62.7 26.2 %copy-start.142 = (f32[64]{0:T(128)}, f32[64]{0:T(128)S(1)}, u32[]{:S(2)}) copy-start(f32[64]{0:T(128)S(1)} %get-tuple-element.168) | copy-start | bytes 772
  65.6 25.4 %copy-start.146 = (f32[32]{0:T(128)}, f32[32]{0:T(128)S(1)}, u32[]{:S(2)}) copy-start(f32[32]{0:T(128)S(1)} %get-tuple-element.162) | copy-start | bytes 388
  67.1 33.6 %copy-start.150 = (f32[32]{0:T(128)}, f32[32]{0:T(128)S(1)}, u32[]{:S(2)}) copy-start(f32[32]{0:T(128)S(1)} %get-tuple-element.164) | copy-start | bytes 388
  71.5 31.3 %copy-start.154 = (f32[16]{0:T(128)}, f32[16]{0:T(128)S(1)}, u32[]{:S(2)}) copy-start(f32[16]{0:T(128)S(1)} %get-tuple-element.158) | copy-start | bytes 196
  73.0 33.5 %copy-start.158 = (f32[16]{0:T(128)}, f32[16]{0:T(128)S(1)}, u32[]{:S(2)}) copy-start(f32[16]{0:T(128)S(1)} %get-tuple-element.160) | copy-start | bytes 196
  77.1 31.5 %copy-start.162 = (f32[8]{0:T(128)}, f32[8]{0:T(128)S(1)}, u32[]{:S(2)}) copy-start(f32[8]{0:T(128)S(1)} %get-tuple-element.154) | copy-start | bytes 100
  78.7 33.8 %copy-start.166 = (f32[8]{0:T(128)}, f32[8]{0:T(128)S(1)}, u32[]{:S(2)}) copy-start(f32[8]{0:T(128)S(1)} %get-tuple-element.156) | copy-start | bytes 100
  87.9 87.8 %copy-start.18 = (f32[2048]{0:T(1024)}, f32[2048]{0:T(1024)S(1)}, u32[]{:S(2)}) copy-start(f32[2048]{0:T(1024)S(1)} %fusion.54) | copy-start | bytes 24580
  88.7 78.8 %copy-start.58 = (f32[256]{0:T(256)}, f32[256]{0:T(256)S(1)}, u32[]{:S(2)}) copy-start(f32[256]{0:T(256)S(1)} %slice.2339) | copy-start | bytes 3076
  89.2 78.4 %copy-start.62 = (f32[256]{0:T(256)}, f32[256]{0:T(256)S(1)}, u32[]{:S(2)}) copy-start(f32[256]{0:T(256)S(1)} %slice.2355) | copy-start | bytes 3076
  89.7 77.9 %copy-start.60 = (f32[256]{0:T(256)}, f32[256]{0:T(256)S(1)}, u32[]{:S(2)}) copy-start(f32[256]{0:T(256)S(1)} %slice.2345) | copy-start | bytes 3076
  90.0 68.3 %copy-start.80 = (f32[256]{0:T(256)}, f32[256]{0:T(256)S(1)}, u32[]{:S(2)}) copy-start(f32[256]{0:T(256)S(1)} %get-tuple-element.216) | copy-start | bytes 3076
  91.2 67.2 %copy-start.82 = (f32[256]{0:T(256)}, f32[256]{0:T(256)S(1)}, u32[]{:S(2)}) copy-start(f32[256]{0:T(256)S(1)} %get-tuple-element.218) | copy-start | bytes 3076
  95.4 63.3 %copy-start.134 = (f32[128]{0:T(128)}, f32[128]{0:T(128)S(1)}, u32[]{:S(2)}) copy-start(f32[128]{0:T(128)S(1)} %get-tuple-element.212) | copy-start | bytes 1540
  102.0 57.7 %copy-start.92 = (f32[64]{0:T(128)}, f32[64]{0:T(128)S(1)}, u32[]{:S(2)}) copy-start(f32[64]{0:T(128)S(1)} %get-tuple-element.208) | copy-start | bytes 772
  103.5 56.2 %copy-start.94 = (f32[64]{0:T(128)}, f32[64]{0:T(128)S(1)}, u32[]{:S(2)}) copy-start(f32[64]{0:T(128)S(1)} %get-tuple-element.210) | copy-start | bytes 772
  107.9 52.0 %copy-start.97 = (f32[32]{0:T(128)}, f32[32]{0:T(128)S(1)}, u32[]{:S(2)}) copy-start(f32[32]{0:T(128)S(1)} %get-tuple-element.204) | copy-start | bytes 388
  109.4 50.5 %copy-start.100 = (f32[32]{0:T(128)}, f32[32]{0:T(128)S(1)}, u32[]{:S(2)}) copy-start(f32[32]{0:T(128)S(1)} %get-tuple-element.206) | copy-start | bytes 388
  113.8 46.2 %copy-start.103 = (f32[16]{0:T(128)}, f32[16]{0:T(128)S(1)}, u32[]{:S(2)}) copy-start(f32[16]{0:T(128)S(1)} %get-tuple-element.200) | copy-start | bytes 196
  115.4 44.7 %copy-start.106 = (f32[16]{0:T(128)}, f32[16]{0:T(128)S(1)}, u32[]{:S(2)}) copy-start(f32[16]{0:T(128)S(1)} %get-tuple-element.202) | copy-start | bytes 196
  119.7 40.4 %copy-start.110 = (f32[8]{0:T(128)}, f32[8]{0:T(128)S(1)}, u32[]{:S(2)}) copy-start(f32[8]{0:T(128)S(1)} %get-tuple-element.196) | copy-start | bytes 100
  121.2 39.0 %copy-start.114 = (f32[8]{0:T(128)}, f32[8]{0:T(128)S(1)}, u32[]{:S(2)}) copy-start(f32[8]{0:T(128)S(1)} %get-tuple-element.198) | copy-start | bytes 100
  125.5 34.7 %copy-start.118 = (f32[4]{0:T(128)}, f32[4]{0:T(128)S(1)}, u32[]{:S(2)}) copy-start(f32[4]{0:T(128)S(1)} %get-tuple-element.192) | copy-start | bytes 52
  127.1 33.2 %copy-start.122 = (f32[4]{0:T(128)}, f32[4]{0:T(128)S(1)}, u32[]{:S(2)}) copy-start(f32[4]{0:T(128)S(1)} %get-tuple-element.194) | copy-start | bytes 52
  129.9 27.8 %copy-start.21 = (f32[1024]{0:T(1024)}, f32[1024]{0:T(1024)S(1)}, u32[]{:S(2)}) copy-start(f32[1024]{0:T(1024)S(1)} %fusion.59) | copy-start | bytes 12292
  147.6 22.4 %copy-start.35 = (f32[14]{0:T(128)}, f32[14]{0:T(128)S(1)}, u32[]{:S(2)}) copy-start(f32[14]{0:T(128)S(1)} %and_convert_fusion.1) | copy-start | bytes 172
  202.1 6.9 %collective-permute-start.4 = (f32[3,3,2048]{2,1,0:T(4,128)S(1)}, f32[3,3,2048]{2,1,0:T(4,128)S(1)}, u32[]{:S(2)}, u32[]{:S(2)}) collective-permute-start(f32[3,3,2048]{2,1,0:T(4,128)S(1)} %get-tuple-element.247), channel_id=1, source_target_pairs={{0,1},{1,2},{2,3},{3,4},{4,5},{5,6},{6,7},{8,9},{9,10},{10,11},{11... | collective-permute-start | bytes 221192 | tf_op jit(solution)/shard_map/ppermute | solution.py:22
  206.6 6.8 %collective-permute-start.5 = (f32[3,3,2048]{2,1,0:T(4,128)S(1)}, f32[3,3,2048]{2,1,0:T(4,128)S(1)}, u32[]{:S(2)}, u32[]{:S(2)}) collective-permute-start(f32[3,3,2048]{2,1,0:T(4,128)S(1)} %get-tuple-element.248), channel_id=1, source_target_pairs={{1,0},{2,1},{3,2},{4,3},{5,4},{6,5},{7,6},{9,8},{10,9},{11,10},{12... | collective-permute-start | bytes 221192 | tf_op jit(solution)/shard_map/ppermute | solution.py:23
  243.6 4.4 %collective-permute-start.6 = (f32[3,3,2048]{2,1,0:T(4,128)S(1)}, f32[3,3,2048]{2,1,0:T(4,128)S(1)}, u32[]{:S(2)}, u32[]{:S(2)}) collective-permute-start(f32[3,3,2048]{2,1,0:T(4,128)S(1)} %get-tuple-element.242), channel_id=1, source_target_pairs={{0,1},{1,2},{2,3},{3,4},{4,5},{5,6},{6,7},{8,9},{9,10},{10,11},{11... | collective-permute-start | bytes 221192 | tf_op jit(solution)/shard_map/ppermute | solution.py:22
  245.6 6.8 %collective-permute-start.7 = (f32[3,3,2048]{2,1,0:T(4,128)S(1)}, f32[3,3,2048]{2,1,0:T(4,128)S(1)}, u32[]{:S(2)}, u32[]{:S(2)}) collective-permute-start(f32[3,3,2048]{2,1,0:T(4,128)S(1)} %get-tuple-element.243), channel_id=1, source_target_pairs={{1,0},{2,1},{3,2},{4,3},{5,4},{6,5},{7,6},{9,8},{10,9},{11,10},{12... | collective-permute-start | bytes 221192 | tf_op jit(solution)/shard_map/ppermute | solution.py:23
  312.7 23.4 %copy-start.36 = (f32[14]{0:T(128)S(1)}, f32[14]{0:T(128)}, u32[]{:S(2)}) copy-start(f32[14]{0:T(128)} %copy-done.35) | copy-start | bytes 172
  312.7 23.6 %copy-start.22 = (f32[1024]{0:T(1024)S(1)}, f32[1024]{0:T(1024)}, u32[]{:S(2)}) copy-start(f32[1024]{0:T(1024)} %copy-done.21) | copy-start | bytes 12292
  323.0 5.4 %collective-permute-start.8 = (f32[3,8,1024]{2,1,0:T(8,128)S(1)}, f32[3,8,1024]{2,1,0:T(8,128)S(1)}, u32[]{:S(2)}, u32[]{:S(2)}) collective-permute-start(f32[3,8,1024]{2,1,0:T(8,128)S(1)} %fusion.19), channel_id=1, source_target_pairs={{0,8},{8,16},{16,24},{1,9},{9,17},{17,25},{2,10},{10,18},{18,26},{... | collective-permute-start | bytes 294920 | tf_op jit(solution)/shard_map/ppermute | solution.py:31
  328.4 6.7 %collective-permute-start.10 = (f32[3,3,1024]{2,1,0:T(4,128)S(1)}, f32[3,3,1024]{2,1,0:T(4,128)S(1)}, u32[]{:S(2)}, u32[]{:S(2)}) collective-permute-start(f32[3,3,1024]{2,1,0:T(4,128)S(1)} %get-tuple-element.317), channel_id=1, source_target_pairs={{1,0},{2,1},{3,2},{4,3},{5,4},{6,5},{7,6},{9,8},{10,9},{11,10},{12... | collective-permute-start | bytes 110600 | tf_op jit(solution)/shard_map/ppermute | solution.py:23
  330.4 5.7 %collective-permute-start.9 = (f32[3,3,1024]{2,1,0:T(4,128)S(1)}, f32[3,3,1024]{2,1,0:T(4,128)S(1)}, u32[]{:S(2)}, u32[]{:S(2)}) collective-permute-start(f32[3,3,1024]{2,1,0:T(4,128)S(1)} %get-tuple-element.316), channel_id=1, source_target_pairs={{0,1},{1,2},{2,3},{3,4},{4,5},{5,6},{6,7},{8,9},{9,10},{10,11},{11... | collective-permute-start | bytes 110600 | tf_op jit(solution)/shard_map/ppermute | solution.py:22
  349.9 6.2 %collective-permute-start.11 = (f32[3,8,1024]{2,1,0:T(8,128)S(1)}, f32[3,8,1024]{2,1,0:T(8,128)S(1)}, u32[]{:S(2)}, u32[]{:S(2)}) collective-permute-start(f32[3,8,1024]{2,1,0:T(8,128)S(1)} %fusion.18), channel_id=1, source_target_pairs={{0,8},{8,16},{16,24},{1,9},{9,17},{17,25},{2,10},{10,18},{18,26},{... | collective-permute-start | bytes 294920 | tf_op jit(solution)/shard_map/ppermute | solution.py:31
  356.2 7.5 %collective-permute-start.12 = (f32[3,3,1024]{2,1,0:T(4,128)S(1)}, f32[3,3,1024]{2,1,0:T(4,128)S(1)}, u32[]{:S(2)}, u32[]{:S(2)}) collective-permute-start(f32[3,3,1024]{2,1,0:T(4,128)S(1)} %get-tuple-element.314), channel_id=1, source_target_pairs={{0,1},{1,2},{2,3},{3,4},{4,5},{5,6},{6,7},{8,9},{9,10},{10,11},{11... | collective-permute-start | bytes 110600 | tf_op jit(solution)/shard_map/ppermute | solution.py:22
  361.6 6.3 %collective-permute-start.13 = (f32[3,3,1024]{2,1,0:T(4,128)S(1)}, f32[3,3,1024]{2,1,0:T(4,128)S(1)}, u32[]{:S(2)}, u32[]{:S(2)}) collective-permute-start(f32[3,3,1024]{2,1,0:T(4,128)S(1)} %get-tuple-element.315), channel_id=1, source_target_pairs={{1,0},{2,1},{3,2},{4,3},{5,4},{6,5},{7,6},{9,8},{10,9},{11,10},{12... | collective-permute-start | bytes 110600 | tf_op jit(solution)/shard_map/ppermute | solution.py:23
  381.4 5.4 %collective-permute-start.14 = (f32[3,8,1024]{2,1,0:T(8,128)S(1)}, f32[3,8,1024]{2,1,0:T(8,128)S(1)}, u32[]{:S(2)}, u32[]{:S(2)}) collective-permute-start(f32[3,8,1024]{2,1,0:T(8,128)S(1)} %fusion.17), channel_id=1, source_target_pairs={{0,8},{8,16},{16,24},{1,9},{9,17},{17,25},{2,10},{10,18},{18,26},{... | collective-permute-start | bytes 294920 | tf_op jit(solution)/shard_map/ppermute | solution.py:31
  386.8 5.0 %collective-permute-start.15 = (f32[3,3,1024]{2,1,0:T(4,128)S(1)}, f32[3,3,1024]{2,1,0:T(4,128)S(1)}, u32[]{:S(2)}, u32[]{:S(2)}) collective-permute-start(f32[3,3,1024]{2,1,0:T(4,128)S(1)} %get-tuple-element.312), channel_id=1, source_target_pairs={{0,1},{1,2},{2,3},{3,4},{4,5},{5,6},{6,7},{8,9},{9,10},{10,11},{11... | collective-permute-start | bytes 110600 | tf_op jit(solution)/shard_map/ppermute | solution.py:22
  389.8 6.3 %collective-permute-start.16 = (f32[3,3,1024]{2,1,0:T(4,128)S(1)}, f32[3,3,1024]{2,1,0:T(4,128)S(1)}, u32[]{:S(2)}, u32[]{:S(2)}) collective-permute-start(f32[3,3,1024]{2,1,0:T(4,128)S(1)} %get-tuple-element.313), channel_id=1, source_target_pairs={{1,0},{2,1},{3,2},{4,3},{5,4},{6,5},{7,6},{9,8},{10,9},{11,10},{12... | collective-permute-start | bytes 110600 | tf_op jit(solution)/shard_map/ppermute | solution.py:23
  (174 other events, 557.4 us)
where the time goes:
time: 423 us; the launch traced here: 418 us
  local copies, waits for them, and re-layouts  188 us (44%)
  other arithmetic  138 us (33%)
  starting transfers between devices  46.5 us (11%)
  waiting for transfers between devices  31.6 us (7%)
  between operations  13.9 us (3%)
    another operation x132, other arithmetic, reduce_lines(): jnp.stack([solved_even, solved_odd], axis=-1).reshape(leading + (length,))  39 us
    another operation x1, local copies, waits for them, and re-layouts, restrict(): blocks = fields.reshape(planes, row_count // 2, 2, columns // 2, 2)  28.5 us
    ppermute x7, starting transfers between devices, extended(): before = lax.ppermute(last, axis, up)  27.7 us
    reshape x1, local copies, waits for them, and re-layouts, restrict(): blocks = fields.reshape(planes, row_count // 2, 2, columns // 2, 2)  27.6 us
    reduce_sum x2, other arithmetic, restrict(): return 0.25 * jnp.sum(blocks, axis=(2, 4))  20.4 us
    unnamed x447, local copies, waits for them, and re-layouts  19.2 us
    ppermute x7, waiting for transfers between devices, extended(): after = lax.ppermute(first, axis, down)  17.6 us
    another operation x66, local copies, waits for them, and re-layouts, reduce_lines(): jnp.stack([solved_even, solved_odd], axis=-1).reshape(leading + (length,))  16.3 us
  transfers between devices with their start and end apart: 17, of which 9 were waited for; matrix products, arithmetic and copies ran while one was open for 35% of the time, Pallas kernels for 0%

commit v1 on v0

v1 whole, which is shorter than its diff:
```python
import functools

import numpy as np
import jax
import jax.numpy as jnp
from jax import lax
from jax.experimental import pallas as pl
from jax.experimental.pallas import tpu as pltpu
from jax.sharding import PartitionSpec as P

STEPS = 3
FINE_SPACING = 0.05
COARSE_SPACING = 0.1
FINE_STEP = 0.015
COARSE_STEP = 0.045
LANES = 128
SUB = 8
MESH = pl.DeviceIdType.MESH
HIGHEST = lax.Precision.HIGHEST


def line_tables(tiles, fine_tiles, stride, length, spacing, step):
    groups = LANES // fine_tiles
    lane = np.arange(LANES)
    chunk = (lane % fine_tiles) * groups + lane // fine_tiles
    columns = tiles * LANES
    centers = (np.arange(columns) + 0.5) * stride
    depth = (0.9 + 0.3 * np.sin(6.0 * np.pi * centers / length)).reshape(LANES, tiles).T
    beta = depth * depth / 3.0
    b = beta / spacing**2
    mid = 1.0 + 2.0 * b
    last = tiles - 1
    inv = np.zeros_like(b)
    cp = np.zeros_like(b)
    for j in range(last):
        inv[j] = 1.0 / (mid[j] - (b[j] * cp[j - 1] if j else 0.0))
        cp[j] = b[j] * inv[j]
    run = np.ones_like(b)
    for j in range(1, tiles):
        run[j] = run[j - 1] * cp[j - 1]
    p = np.zeros_like(b)
    q = np.zeros_like(b)
    q[last] = 1.0
    for j in range(last - 1, -1, -1):
        p[j] = run[j + 1] + cp[j] * p[j + 1]
        q[j] = cp[j] * q[j + 1]
    system = np.zeros((LANES, LANES))
    for k in range(LANES):
        system[k, k] = mid[last, k] - b[last, k] * q[last - 1, k]
        if k:
            system[k, k - 1] = -b[last, k] * p[last - 1, k]
        if k + 1 < LANES:
            system[k, k] -= b[last, k] * p[0, k + 1]
            system[k, k + 1] = -b[last, k] * q[0, k + 1]
    solve = np.linalg.inv(system).T
    weights = np.zeros((2 * LANES, 2 * LANES))
    weights[:LANES, :LANES] = solve
    weights[LANES + 1 :, :LANES] = solve[:-1] * b[last, :-1, None]
    weights[:, LANES + 1 :] = weights[:, : LANES - 1]
    both = np.concatenate([chunk, LANES + chunk])
    weights = weights[both][:, both]
    slope = step * depth / (2.0 * spacing)
    weight = beta / (spacing**2 + 4.0 * beta)
    inv[last] = b[last]
    rows = np.stack([inv, cp, run, slope, weight])[:, :, chunk]
    return rows.astype(np.float32), weights.astype(np.float32)


def relaid(tiles):
    tiles = list(tiles)
    lane = lax.broadcasted_iota(jnp.int32, tiles[0].shape, 1)
    bit = 1
    while bit < len(tiles):
        keep = (lane & bit) == 0
        for t in range(len(tiles)):
            if t & bit == 0:
                a, b = tiles[t], tiles[t | bit]
                tiles[t] = jnp.where(keep, a, pltpu.roll(b, bit, 1))
                tiles[t | bit] = jnp.where(keep, pltpu.roll(a, LANES - bit, 1), b)
        bit *= 2
    return tiles


def wave(state, height, held, rows, weights, tiles, fine_tiles, factor, inside):
    count = state.shape[2]
    lane = lax.broadcasted_iota(jnp.int32, (count, LANES), 1)

    def chunk_before(x):
        wrapped = jnp.where(lane == 0, 0.0, pltpu.roll(x, fine_tiles + 1, 1))
        return jnp.where(lane >= fine_tiles, pltpu.roll(x, fine_tiles, 1), wrapped)

    def chunk_after(x):
        wrapped = jnp.where(lane == LANES - 1, 0.0, pltpu.roll(x, LANES - fine_tiles - 1, 1))
        return jnp.where(lane < LANES - fine_tiles, pltpu.roll(x, LANES - fine_tiles, 1), wrapped)

    def below(x):
        return pltpu.roll(x, count - 1, 0)

    def above(x):
        return pltpu.roll(x, 1, 0)

    def across(load, j):
        right = load(j + 1) if j + 1 < tiles else chunk_after(load(0))
        left = load(j - 1) if j else chunk_before(load(tiles - 1))
        return right - left

    def table(kind, j):
        return rows[kind, pl.ds(j, 1), :]

    for j in range(tiles):
        flux_y = state[2, j]
        spread = across(lambda i: state[1, i], j) + (below(flux_y) - above(flux_y))
        height[j] = (state[0, j] - factor * spread) * inside
    total = None
    inner = None
    for j in range(tiles):
        middle = height[j]
        slope = table(3, j)
        force_x = state[1, j] - slope * across(lambda i: height[i], j)
        force_y = state[2, j] - slope * (below(middle) - above(middle))
        force = jnp.concatenate([force_x, force_y], axis=0)
        if j == tiles - 1:
            edge = force + table(0, j) * inner
        elif j == 0:
            inner = force * table(0, j)
            total = inner
            held[j] = inner
        else:
            inner = force * table(0, j) + table(1, j) * inner
            total = total + table(2, j) * inner
            held[j] = inner
    met = jnp.dot(
        jnp.concatenate([edge, total], axis=1),
        weights[...],
        precision=HIGHEST,
        preferred_element_type=jnp.float32,
    )
    value = met[:, :LANES]
    before = met[:, LANES:]
    for j in range(tiles - 1, -1, -1):
        if j < tiles - 1:
            value = held[j] + table(2, j + 1) * before + table(1, j) * value
        weight = table(4, j)
        for part in range(2):
            trial = value[part * count : (part + 1) * count] * inside
            change = trial - state[1 + part, j]
            curve = below(change) - 2.0 * change + above(change)
            state[1 + part, j] = (trial + weight * curve) * inside
        state[0, j] = height[j]


def kernel(
    tile_count, slices, x_ref, fine_rows, fine_weights, coarse_rows, coarse_weights, out_ref,
    up_pair, up_y, down_pair, down_y, state, height, held,
    c_state, c_height, c_held, start, end, arrived, own, above_own, below_own, leaving,
    send, recv,
):
    cut = lax.axis_index("cuts")
    tile = lax.axis_index("tile")
    has_up = tile > 0
    has_down = tile < tile_count - 1
    planes, row_count, columns = x_ref.shape
    tiles = columns // LANES
    half = tiles // 2
    groups = row_count // SUB
    total_rows = row_count * tile_count

    barrier = pltpu.get_barrier_semaphore()
    near = [
        (has_up, {"tile": tile - 1}),
        (has_down, {"tile": tile + 1}),
        (cut > 0, {"cuts": cut - 1}),
        (cut < slices - 1, {"cuts": cut + 1}),
    ]
    for exists, place in near:
        @pl.when(exists)
        def _():
            pl.semaphore_signal(barrier, inc=1, device_id=place, device_id_type=MESH)
    pl.semaphore_wait(barrier, sum(exists.astype(jnp.int32) for exists, _ in near))

    def remote(source, target, which, place):
        return pltpu.make_async_remote_copy(
            src_ref=source, dst_ref=target, send_sem=send.at[which], recv_sem=recv.at[which],
            device_id=place, device_id_type=MESH,
        )

    to_up = {"tile": tile - 1}
    to_down = {"tile": tile + 1}
    two = pl.ds(0, 2)
    going_down = [
        remote(x_ref.at[two, pl.ds(row_count - SUB, SUB)], up_pair, 0, to_down),
        remote(x_ref.at[2, pl.ds(row_count - 2 * SUB, 2 * SUB)], up_y, 1, to_down),
    ]
    going_up = [
        remote(x_ref.at[two, pl.ds(0, SUB)], down_pair, 2, to_up),
        remote(x_ref.at[2, pl.ds(0, 2 * SUB)], down_y, 3, to_up),
    ]

    @pl.when(has_down)
    def _():
        for copy in going_down:
            copy.start()

    @pl.when(has_up)
    def _():
        for copy in going_up:
            copy.start()

    def place_rows(values, plane, row):
        parts = relaid([values[:, t * LANES : (t + 1) * LANES] for t in range(tiles)])
        for j in range(tiles):
            state[plane, j, pl.ds(row, SUB), :] = parts[j]

    tail = SUB * (groups + 2)
    for plane in range(planes):
        for group in range(groups):
            place_rows(x_ref[plane, pl.ds(group * SUB, SUB), :], plane, SUB * (group + 1))
    for plane in range(planes - 1):
        for j in range(tiles):
            state[plane, j, pl.ds(tail, SUB), :] = jnp.zeros((SUB, LANES), jnp.float32)

    def restrict(target):
        for plane in range(planes):
            for j in range(half):
                parts = [
                    state[plane, 2 * j + k, pl.ds(SUB + r, row_count // 2, stride=2), :]
                    for r in range(2)
                    for k in range(2)
                ]
                target[plane, j] = 0.25 * ((parts[0] + parts[1]) + (parts[2] + parts[3]))

    restrict(start)

    @pl.when(has_up)
    def _():
        for copy in going_down:
            copy.wait_recv()

    @pl.when(jnp.logical_not(has_up))
    def _():
        up_pair[...] = jnp.zeros_like(up_pair)
        up_y[...] = jnp.zeros_like(up_y)
        above_own[...] = jnp.zeros_like(above_own)

    @pl.when(has_down)
    def _():
        for copy in going_up:
            copy.wait_recv()

    @pl.when(jnp.logical_not(has_down))
    def _():
        down_pair[...] = jnp.zeros_like(down_pair)
        down_y[...] = jnp.zeros_like(down_y)
        below_own[...] = jnp.zeros_like(below_own)

    for plane in range(2):
        place_rows(up_pair[plane], plane, 0)
        place_rows(down_pair[plane], plane, tail - SUB)
    place_rows(up_y[pl.ds(SUB, SUB), :], 2, 0)
    place_rows(down_y[pl.ds(0, SUB), :], 2, tail - SUB)
    first = lax.broadcasted_iota(jnp.int32, (SUB, columns), 0) < SUB // 2
    mixed = jnp.where(first, down_y[pl.ds(SUB, SUB), :], up_y[pl.ds(0, SUB), :])
    place_rows(mixed, 2, tail)

    def mask(count, lead, total, origin):
        at = lax.broadcasted_iota(jnp.int32, (count, LANES), 0)
        row = jnp.where(at >= count - SUB // 2, at - count, at) - lead + origin
        return ((row >= 0) & (row < total)).astype(jnp.float32)

    fine_inside = mask(tail + SUB, SUB, total_rows, tile * row_count)

    def fine_step(step, carry):
        wave(
            state, height, held, fine_rows, fine_weights, tiles, tiles,
            FINE_STEP / (2.0 * FINE_SPACING), fine_inside,
        )
        return carry

    lax.fori_loop(0, STEPS, fine_step, 0)
    restrict(end)

    coarse_count = row_count // 2
    onward = remote(leaving, arrived, 4, {"cuts": cut + 1})
    own_down = remote(own, above_own, 5, to_down)
    own_up = remote(own, below_own, 6, to_up)

    @pl.when(cut == 0)
    def _():
        leaving[...] = end[...]

    @pl.when(cut > 0)
    def _():
        onward.wait_recv()
        own[...] = arrived[...] - start[...]

        @pl.when(has_down)
        def _():
            own_down.start()

        @pl.when(has_up)
        def _():
            own_up.start()

        @pl.when(has_up)
        def _():
            own_down.wait_recv()

        @pl.when(has_down)
        def _():
            own_up.wait_recv()

        near_rows = lax.broadcasted_iota(jnp.int32, (coarse_count, LANES), 0) < coarse_count // 2
        for plane in range(planes):
            for j in range(half):
                c_state[plane, j, pl.ds(0, coarse_count), :] = own[plane, j]
                c_state[plane, j, pl.ds(coarse_count, coarse_count), :] = jnp.where(
                    near_rows, below_own[plane, j], above_own[plane, j]
                )
        coarse_inside = mask(2 * coarse_count, 0, total_rows // 2, tile * coarse_count)
        wave(
            c_state, c_height, c_held, coarse_rows, coarse_weights, half, tiles,
            COARSE_STEP / (2.0 * COARSE_SPACING), coarse_inside,
        )
        for plane in range(planes):
            for j in range(half):
                leaving[plane, j] = c_state[plane, j, pl.ds(0, coarse_count), :] + end[plane, j]

    @pl.when(cut < slices - 1)
    def _():
        onward.start()

    @pl.when(cut > 0)
    def _():
        for plane in range(planes):
            for j in range(tiles):
                gain = c_state[plane, j // 2, pl.ds(0, coarse_count), :]
                for r in range(2):
                    at = pl.ds(SUB + r, coarse_count, stride=2)
                    state[plane, j, at, :] = state[plane, j, at, :] + gain

    for plane in range(planes):
        for group in range(groups):
            rows = pl.ds(SUB * (group + 1), SUB)
            parts = relaid([state[plane, j, rows, :] for j in range(tiles)])
            for t in range(tiles):
                out_ref[plane, pl.ds(group * SUB, SUB), pl.ds(t * LANES, LANES)] = parts[t]

    @pl.when(has_down)
    def _():
        for copy in going_down:
            copy.wait_send()

    @pl.when(has_up)
    def _():
        for copy in going_up:
            copy.wait_send()

    @pl.when(cut < slices - 1)
    def _():
        onward.wait_send()

    @pl.when((cut > 0) & has_down)
    def _():
        own_down.wait_send()

    @pl.when((cut > 0) & has_up)
    def _():
        own_up.wait_send()


def per_device(tile_count, slices, start_states):
    fields = start_states[0]
    planes, row_count, columns = fields.shape
    tiles = columns // LANES
    half = tiles // 2
    fine = line_tables(tiles, tiles, 1.0, columns, FINE_SPACING, FINE_STEP)
    coarse = line_tables(half, tiles, 2.0, columns, COARSE_SPACING, COARSE_STEP)
    fine_count = row_count + 3 * SUB
    coarse_count = row_count // 2
    f32 = jnp.float32
    slab = pltpu.VMEM((planes, half, coarse_count, LANES), f32)
    out = pl.pallas_call(
        functools.partial(kernel, tile_count, slices),
        out_shape=jax.ShapeDtypeStruct(fields.shape, f32),
        in_specs=[pl.BlockSpec(memory_space=pltpu.VMEM)] * 5,
        out_specs=pl.BlockSpec(memory_space=pltpu.VMEM),
        scratch_shapes=[
            pltpu.VMEM((2, SUB, columns), f32),
            pltpu.VMEM((2 * SUB, columns), f32),
            pltpu.VMEM((2, SUB, columns), f32),
            pltpu.VMEM((2 * SUB, columns), f32),
            pltpu.VMEM((planes, tiles, fine_count, LANES), f32),
            pltpu.VMEM((tiles, fine_count, LANES), f32),
            pltpu.VMEM((tiles, 2 * fine_count, LANES), f32),
            pltpu.VMEM((planes, half, 2 * coarse_count, LANES), f32),
            pltpu.VMEM((half, 2 * coarse_count, LANES), f32),
            pltpu.VMEM((half, 4 * coarse_count, LANES), f32),
        ]
        + [slab] * 7
        + [pltpu.SemaphoreType.DMA((7,)), pltpu.SemaphoreType.DMA((7,))],
        compiler_params=pltpu.CompilerParams(collective_id=0, has_side_effects=True),
    )(fields, *[jnp.asarray(a) for a in fine + coarse])
    return out[None]


def solution(mesh):
    spec = P("cuts", None, "tile", None)
    body = functools.partial(per_device, mesh.shape["tile"], mesh.shape["cuts"])
    return jax.shard_map(body, mesh=mesh, in_specs=(spec,), out_specs=spec, check_vma=False)
```

time: 423 us -> 39.8 us (0.09); the launches traced: 418 us -> 39.7 us
  local copies, waits for them, and re-layouts: 188 us -> 1.77 us
  other arithmetic: 138 us -> 0 us
  starting transfers between devices: 46.5 us -> 0 us
  Pallas kernels: 0 us -> 37.9 us
  waiting for transfers between devices: 31.6 us -> 0 us
  between operations: 13.9 us -> 0.01 us
    slice x332 -> x0, local copies, waits for them, and re-layouts: 82 us -> none  [the longest x19 10.1 us: reduce_lines(): upper_after = jnp.concatenate([upper_even[1:], no_more])]
    ppermute x17 -> x0, starting transfers between devices: 46.5 us -> none  [the longest x7 27.7 us: extended(): before = lax.ppermute(last, axis, up)]
    another operation x72 -> x0, local copies, waits for them, and re-layouts: 45 us -> none  [the longest x1 28.5 us: restrict(): blocks = fields.reshape(planes, row_count // 2, 2, columns // 2, 2)]
    another operation x134 -> x0, other arithmetic: 42.2 us -> none  [the longest x132 39 us: reduce_lines(): jnp.stack([solved_even, solved_odd], axis=-1).reshape(leading + (length,))]
    pallas_call x0 -> x1, Pallas kernels: none -> 37.9 us  [per_device(): pl.pallas_call(functools.partial(kernel, tile_count, slices), out_shape=j...]
    ppermute x17 -> x0, waiting for transfers between devices: 31.6 us -> none  [the longest x7 17.6 us: extended(): after = lax.ppermute(first, axis, down)]
    reshape x7 -> x0, local copies, waits for them, and re-layouts: 29.6 us -> none  [the longest x1 27.6 us: restrict(): blocks = fields.reshape(planes, row_count // 2, 2, columns // 2, 2)]
    mul x54 -> x0, other arithmetic: 27.6 us -> none  [the longest x19 8.33 us: reduce_lines(): new_lower = alpha * lower_even]
  transfers between devices with their start and end apart: 17 -> 0, of which waited for: 9 -> 0; matrix products, arithmetic and copies ran while one was open for 35% -> 0% of each run, Pallas kernels for 0% -> 0%
where the time goes in v1:
time: 39.8 us; the launch traced here: 39.7 us
  Pallas kernels  37.9 us (95%)
  local copies, waits for them, and re-layouts  1.77 us (4%)
    pallas_call x1, Pallas kernels, per_device(): pl.pallas_call(functools.partial(kernel, tile_count, slices), out_shape=j...  37.9 us
    unnamed x1, local copies, waits for them, and re-layouts  1.77 us

profile of v1, /device:TPU:27, one launch (start us, length us, event | category | flops | bytes accessed | tf_op | source)
XLA Modules:
  0.0 39.7 jit_solution(4826814258462709326)
XLA Ops:
  0.0 37.9 %shard_map.55 = f32[3,16,2048]{2,1,0:T(8,128)} custom-call(f32[3,16,2048]{2,1,0:T(8,128)} %bitcast.3, f32[5,16,128]{2,1,0:T(8,128)} %constant.8.clone.fine_rows, f32[256,256]{1,0:T(8,128)} %constant.9.clone.fine_weights, f32[5,8,128]{2,1,0:T(8,128)} %constant.10.clone.coarse_rows, f32[256,256]{1,0:T(8,128)} %constant.11.clone.coarse_weights), custom_call_target="tpu_custom_call" | custom-call | tf_op jit(solution)/shard_map/pallas_call | solution.py:382
  37.9 1.8 %copy.7 = f32[1,3,16,2048]{3,2,1,0:T(8,128)} copy(f32[1,3,16,2048]{3,2,1,0:T(8,128)} %bitcast.2) | data formatting | bytes 786432

commit v2 on v1

--- a/solution.py
+++ b/solution.py
@@ -15,6 +15,7 @@
 COARSE_STEP = 0.045
 LANES = 128
 SUB = 8
+HALO = 3
 MESH = pl.DeviceIdType.MESH
 HIGHEST = lax.Precision.HIGHEST
 
@@ -150,61 +151,73 @@
 
 
 def kernel(
-    tile_count, slices, x_ref, fine_rows, fine_weights, coarse_rows, coarse_weights, out_ref,
-    up_pair, up_y, down_pair, down_y, state, height, held,
-    c_state, c_height, c_held, start, end, arrived, own, above_own, below_own, leaving,
-    send, recv,
+    tile_count, slices, x_hbm, fine_rows_hbm, fine_weights_hbm, coarse_rows_hbm,
+    coarse_weights_hbm, out_ref,
+    x_ref, fine_rows, fine_weights, coarse_rows, coarse_weights,
+    up_main, down_main, edge, up_edge, down_edge, state, height, held,
+    c_state, c_height, c_held, start, end, arrived, leaving, low, far_start, above_in, below_in,
+    local, send, recv,
 ):
     cut = lax.axis_index("cuts")
     tile = lax.axis_index("tile")
     has_up = tile > 0
     has_down = tile < tile_count - 1
+    has_before = cut > 0
+    has_after = cut < slices - 1
     planes, row_count, columns = x_ref.shape
     tiles = columns // LANES
     half = tiles // 2
     groups = row_count // SUB
     total_rows = row_count * tile_count
+    coarse_count = row_count // 2
+
+    pairs = [
+        (x_hbm, x_ref), (fine_rows_hbm, fine_rows), (fine_weights_hbm, fine_weights),
+        (coarse_rows_hbm, coarse_rows), (coarse_weights_hbm, coarse_weights),
+    ]
+    loads = [pltpu.make_async_copy(a, b, local.at[i]) for i, (a, b) in enumerate(pairs)]
+    for load in loads:
+        load.start()
 
     barrier = pltpu.get_barrier_semaphore()
-    near = [
-        (has_up, {"tile": tile - 1}),
-        (has_down, {"tile": tile + 1}),
-        (cut > 0, {"cuts": cut - 1}),
-        (cut < slices - 1, {"cuts": cut + 1}),
-    ]
-    for exists, place in near:
+    near = [(has_up, cut, tile - 1), (has_down, cut, tile + 1)]
+    for there, other in ((has_before, cut - 1), (has_after, cut + 1)):
+        near.append((there, other, tile))
+        near.append((there & has_up, other, tile - 1))
+        near.append((there & has_down, other, tile + 1))
+    for exists, to_cut, to_tile in near:
         @pl.when(exists)
         def _():
-            pl.semaphore_signal(barrier, inc=1, device_id=place, device_id_type=MESH)
-    pl.semaphore_wait(barrier, sum(exists.astype(jnp.int32) for exists, _ in near))
-
-    def remote(source, target, which, place):
+            pl.semaphore_signal(
+                barrier, inc=1, device_id=(to_cut, to_tile), device_id_type=MESH
+            )
+    pl.semaphore_wait(barrier, sum(exists.astype(jnp.int32) for exists, _, _ in near))
+
+    def remote(source, target, which, to_cut, to_tile):
         return pltpu.make_async_remote_copy(
             src_ref=source, dst_ref=target, send_sem=send.at[which], recv_sem=recv.at[which],
-            device_id=place, device_id_type=MESH,
+            device_id=(to_cut, to_tile), device_id_type=MESH,
         )
 
-    to_up = {"tile": tile - 1}
-    to_down = {"tile": tile + 1}
-    two = pl.ds(0, 2)
-    going_down = [
-        remote(x_ref.at[two, pl.ds(row_count - SUB, SUB)], up_pair, 0, to_down),
-        remote(x_ref.at[2, pl.ds(row_count - 2 * SUB, 2 * SUB)], up_y, 1, to_down),
-    ]
-    going_up = [
-        remote(x_ref.at[two, pl.ds(0, SUB)], down_pair, 2, to_up),
-        remote(x_ref.at[2, pl.ds(0, 2 * SUB)], down_y, 3, to_up),
-    ]
+    one = pl.ds(0, 1)
+    main_down = remote(
+        x_hbm.at[:, pl.ds(row_count - SUB, SUB)], up_main, 0, cut, tile + 1
+    )
+    edge_down = remote(edge.at[one], up_edge.at[one], 1, cut, tile + 1)
+    main_up = remote(x_hbm.at[:, pl.ds(0, SUB)], down_main, 2, cut, tile - 1)
+    edge_up = remote(x_hbm.at[planes - 1, pl.ds(SUB, 1)], down_edge.at[one], 3, cut, tile - 1)
 
     @pl.when(has_down)
     def _():
-        for copy in going_down:
-            copy.start()
+        main_down.start()
 
     @pl.when(has_up)
     def _():
-        for copy in going_up:
-            copy.start()
+        edge_up.start()
+        main_up.start()
+
+    loads[0].wait()
+    edge[one, :] = x_ref[planes - 1, pl.ds(row_count - SUB - 1, 1), :]
 
     def place_rows(values, plane, row):
         parts = relaid([values[:, t * LANES : (t + 1) * LANES] for t in range(tiles)])
@@ -212,55 +225,73 @@
             state[plane, j, pl.ds(row, SUB), :] = parts[j]
 
     tail = SUB * (groups + 2)
-    for plane in range(planes):
+    for plane in range(planes - 1):
         for group in range(groups):
             place_rows(x_ref[plane, pl.ds(group * SUB, SUB), :], plane, SUB * (group + 1))
-    for plane in range(planes - 1):
         for j in range(tiles):
             state[plane, j, pl.ds(tail, SUB), :] = jnp.zeros((SUB, LANES), jnp.float32)
 
-    def restrict(target):
-        for plane in range(planes):
-            for j in range(half):
-                parts = [
-                    state[plane, 2 * j + k, pl.ds(SUB + r, row_count // 2, stride=2), :]
-                    for r in range(2)
-                    for k in range(2)
-                ]
-                target[plane, j] = 0.25 * ((parts[0] + parts[1]) + (parts[2] + parts[3]))
-
-    restrict(start)
+    @pl.when(has_down)
+    def _():
+        edge_down.start()
+
+    for group in range(groups):
+        place_rows(
+            x_ref[planes - 1, pl.ds(group * SUB, SUB), :], planes - 1, SUB * (group + 1)
+        )
+
+    def restricted(plane, j, row, count):
+        parts = [
+            state[plane, 2 * j + k, pl.ds(row + r, count, stride=2), :]
+            for r in range(2)
+            for k in range(2)
+        ]
+        return 0.25 * ((parts[0] + parts[1]) + (parts[2] + parts[3]))
+
+    def each_slab():
+        return [(plane, j) for plane in range(planes) for j in range(half)]
+
+    for plane, j in each_slab():
+        start[plane, j] = restricted(plane, j, SUB, coarse_count)
+    for load in loads[1:]:
+        load.wait()
+
+    @pl.when(jnp.logical_not(has_up))
+    def _():
+        up_main[...] = jnp.zeros_like(up_main)
+        up_edge[...] = jnp.zeros_like(up_edge)
+
+    @pl.when(jnp.logical_not(has_down))
+    def _():
+        down_main[...] = jnp.zeros_like(down_main)
+        down_edge[...] = jnp.zeros_like(down_edge)
 
     @pl.when(has_up)
     def _():
-        for copy in going_down:
-            copy.wait_recv()
-
-    @pl.when(jnp.logical_not(has_up))
-    def _():
-        up_pair[...] = jnp.zeros_like(up_pair)
-        up_y[...] = jnp.zeros_like(up_y)
-        above_own[...] = jnp.zeros_like(above_own)
+        main_down.wait_recv()
+        edge_down.wait_recv()
 
     @pl.when(has_down)
     def _():
-        for copy in going_up:
-            copy.wait_recv()
-
-    @pl.when(jnp.logical_not(has_down))
-    def _():
-        down_pair[...] = jnp.zeros_like(down_pair)
-        down_y[...] = jnp.zeros_like(down_y)
-        below_own[...] = jnp.zeros_like(below_own)
-
-    for plane in range(2):
-        place_rows(up_pair[plane], plane, 0)
-        place_rows(down_pair[plane], plane, tail - SUB)
-    place_rows(up_y[pl.ds(SUB, SUB), :], 2, 0)
-    place_rows(down_y[pl.ds(0, SUB), :], 2, tail - SUB)
-    first = lax.broadcasted_iota(jnp.int32, (SUB, columns), 0) < SUB // 2
-    mixed = jnp.where(first, down_y[pl.ds(SUB, SUB), :], up_y[pl.ds(0, SUB), :])
-    place_rows(mixed, 2, tail)
+        main_up.wait_recv()
+        edge_up.wait_recv()
+
+    for plane in range(planes):
+        place_rows(up_main[plane], plane, 0)
+        place_rows(down_main[plane], plane, tail - SUB)
+    at_row = lax.broadcasted_iota(jnp.int32, (SUB, columns), 0)
+    mixed = jnp.where(
+        at_row == 0,
+        jnp.broadcast_to(down_edge[one, :], (SUB, columns)),
+        jnp.where(
+            at_row == SUB - 1, jnp.broadcast_to(up_edge[one, :], (SUB, columns)), 0.0
+        ),
+    )
+    place_rows(mixed, planes - 1, tail)
+
+    for plane, j in each_slab():
+        far_start[plane, j, pl.ds(0, SUB // 2), :] = restricted(plane, j, tail - SUB, SUB // 2)
+        far_start[plane, j, pl.ds(SUB // 2, SUB // 2), :] = restricted(plane, j, 0, SUB // 2)
 
     def mask(count, lead, total, origin):
         at = lax.broadcasted_iota(jnp.int32, (count, LANES), 0)
@@ -277,59 +308,77 @@
         return carry
 
     lax.fori_loop(0, STEPS, fine_step, 0)
-    restrict(end)
-
-    coarse_count = row_count // 2
-    onward = remote(leaving, arrived, 4, {"cuts": cut + 1})
-    own_down = remote(own, above_own, 5, to_down)
-    own_up = remote(own, below_own, 6, to_up)
+
+    three = pl.ds(0, HALO)
+    part = (slice(None), slice(None), three)
+    to_own = remote(leaving, arrived, 4, cut + 1, tile)
+    to_above = remote(leaving.at[part], below_in.at[part], 5, cut + 1, tile - 1)
+    to_below = remote(low.at[part], above_in.at[part], 6, cut + 1, tile + 1)
+
+    def leave(plane, j, value):
+        leaving[plane, j] = value
+        low[plane, j] = pltpu.roll(value, HALO, 0)
 
     @pl.when(cut == 0)
     def _():
-        leaving[...] = end[...]
-
-    @pl.when(cut > 0)
-    def _():
-        onward.wait_recv()
-        own[...] = arrived[...] - start[...]
+        for plane, j in each_slab():
+            leave(plane, j, restricted(plane, j, SUB, coarse_count))
+
+    @pl.when(has_before)
+    def _():
+        for plane, j in each_slab():
+            end[plane, j] = restricted(plane, j, SUB, coarse_count)
+
+        @pl.when(jnp.logical_not(has_up))
+        def _():
+            above_in[...] = jnp.zeros_like(above_in)
+
+        @pl.when(jnp.logical_not(has_down))
+        def _():
+            below_in[...] = jnp.zeros_like(below_in)
+
+        @pl.when(has_up)
+        def _():
+            to_below.wait_recv()
 
         @pl.when(has_down)
         def _():
-            own_down.start()
-
-        @pl.when(has_up)
-        def _():
-            own_up.start()
-
-        @pl.when(has_up)
-        def _():
-            own_down.wait_recv()
-
-        @pl.when(has_down)
-        def _():
-            own_up.wait_recv()
-
-        near_rows = lax.broadcasted_iota(jnp.int32, (coarse_count, LANES), 0) < coarse_count // 2
-        for plane in range(planes):
-            for j in range(half):
-                c_state[plane, j, pl.ds(0, coarse_count), :] = own[plane, j]
-                c_state[plane, j, pl.ds(coarse_count, coarse_count), :] = jnp.where(
-                    near_rows, below_own[plane, j], above_own[plane, j]
-                )
-        coarse_inside = mask(2 * coarse_count, 0, total_rows // 2, tile * coarse_count)
+            to_above.wait_recv()
+
+        at = lax.broadcasted_iota(jnp.int32, (SUB, LANES), 0)
+        for plane, j in each_slab():
+            around = jnp.where(
+                at < HALO,
+                below_in[plane, j],
+                jnp.where(
+                    at >= SUB - HALO, pltpu.roll(above_in[plane, j], SUB - HALO, 0), 0.0
+                ),
+            )
+            c_state[plane, j, pl.ds(coarse_count, SUB), :] = around - far_start[plane, j]
+        to_own.wait_recv()
+        for plane, j in each_slab():
+            c_state[plane, j, pl.ds(0, coarse_count), :] = arrived[plane, j] - start[plane, j]
+        coarse_inside = mask(coarse_count + SUB, 0, total_rows // 2, tile * coarse_count)
         wave(
             c_state, c_height, c_held, coarse_rows, coarse_weights, half, tiles,
             COARSE_STEP / (2.0 * COARSE_SPACING), coarse_inside,
         )
-        for plane in range(planes):
-            for j in range(half):
-                leaving[plane, j] = c_state[plane, j, pl.ds(0, coarse_count), :] + end[plane, j]
-
-    @pl.when(cut < slices - 1)
-    def _():
-        onward.start()
-
-    @pl.when(cut > 0)
+        for plane, j in each_slab():
+            leave(plane, j, c_state[plane, j, pl.ds(0, coarse_count), :] + end[plane, j])
+
+    @pl.when(has_after & has_up)
+    def _():
+        to_above.start()
+
+    @pl.when(has_after & has_down)
+    def _():
+        to_below.start()
+
+    @pl.when(has_after)
+    def _():
+        to_own.start()
+
+    @pl.when(has_before)
     def _():
         for plane in range(planes):
             for j in range(tiles):
@@ -347,25 +396,25 @@
 
     @pl.when(has_down)
     def _():
-        for copy in going_down:
-            copy.wait_send()
+        main_down.wait_send()
+        edge_down.wait_send()
 
     @pl.when(has_up)
     def _():
-        for copy in going_up:
-            copy.wait_send()
-
-    @pl.when(cut < slices - 1)
-    def _():
-        onward.wait_send()
-
-    @pl.when((cut > 0) & has_down)
-    def _():
-        own_down.wait_send()
-
-    @pl.when((cut > 0) & has_up)
-    def _():
-        own_up.wait_send()
+        main_up.wait_send()
+        edge_up.wait_send()
+
+    @pl.when(has_after & has_up)
+    def _():
+        to_above.wait_send()
+
+    @pl.when(has_after & has_down)
+    def _():
+        to_below.wait_send()
+
+    @pl.when(has_after)
+    def _():
+        to_own.wait_send()
 
 
 def per_device(tile_count, slices, start_states):
@@ -382,13 +431,13 @@
     out = pl.pallas_call(
         functools.partial(kernel, tile_count, slices),
         out_shape=jax.ShapeDtypeStruct(fields.shape, f32),
-        in_specs=[pl.BlockSpec(memory_space=pltpu.VMEM)] * 5,
+        in_specs=[pl.BlockSpec(memory_space=pl.ANY)] * 5,
         out_specs=pl.BlockSpec(memory_space=pltpu.VMEM),
-        scratch_shapes=[
-            pltpu.VMEM((2, SUB, columns), f32),
-            pltpu.VMEM((2 * SUB, columns), f32),
-            pltpu.VMEM((2, SUB, columns), f32),
-            pltpu.VMEM((2 * SUB, columns), f32),
+        scratch_shapes=[pltpu.VMEM(fields.shape, f32)]
+        + [pltpu.VMEM(a.shape, f32) for a in fine + coarse]
+        + [pltpu.VMEM((planes, SUB, columns), f32)] * 2
+        + [pltpu.VMEM((SUB, columns), f32)] * 3
+        + [
             pltpu.VMEM((planes, tiles, fine_count, LANES), f32),
             pltpu.VMEM((tiles, fine_count, LANES), f32),
             pltpu.VMEM((tiles, 2 * fine_count, LANES), f32),
@@ -396,8 +445,12 @@
             pltpu.VMEM((half, 2 * coarse_count, LANES), f32),
             pltpu.VMEM((half, 4 * coarse_count, LANES), f32),
         ]
-        + [slab] * 7
-        + [pltpu.SemaphoreType.DMA((7,)), pltpu.SemaphoreType.DMA((7,))],
+        + [slab] * 8
+        + [
+            pltpu.SemaphoreType.DMA((5,)),
+            pltpu.SemaphoreType.DMA((7,)),
+            pltpu.SemaphoreType.DMA((7,)),
+        ],
         compiler_params=pltpu.CompilerParams(collective_id=0, has_side_effects=True),
     )(fields, *[jnp.asarray(a) for a in fine + coarse])
     return out[None]

time: 39.8 us -> 31 us (0.78)
  Pallas kernels: 37.9 us -> 29 us
    pallas_call x1, Pallas kernels: 37.9 us -> 29 us  [per_device(): pl.pallas_call(functools.partial(kernel, tile_count, slices), out_shape=j...]
where the time goes in v2:
time: 31 us; the launch traced here: 30.8 us
  Pallas kernels  29 us (94%)
  local copies, waits for them, and re-layouts  1.77 us (6%)
    pallas_call x1, Pallas kernels, per_device(): pl.pallas_call(functools.partial(kernel, tile_count, slices), out_shape=j...  29 us
    unnamed x1, local copies, waits for them, and re-layouts  1.77 us

profile of v2, /device:TPU:27, one launch (start us, length us, event | category | flops | bytes accessed | tf_op | source)
XLA Modules:
  0.0 30.8 jit_solution(8389250991291239141)
XLA Ops:
  0.0 29.0 %shard_map.55 = f32[3,16,2048]{2,1,0:T(8,128)} custom-call(f32[3,16,2048]{2,1,0:T(8,128)} %bitcast.3, f32[5,16,128]{2,1,0:T(8,128)} %constant.8.clone.fine_rows_hbm, f32[256,256]{1,0:T(8,128)} %constant.9.clone.fine_weights_hbm, f32[5,8,128]{2,1,0:T(8,128)} %constant.10.clone.coarse_rows_hbm, f32[256,256]{1,0:T(8,128)} %constant.11.clone.coarse_weights_hbm), custom_call_target="tpu_custom_call" | custom-call | tf_op jit(solution)/shard_map/pallas_call | solution.py:431
  29.1 1.8 %copy.7 = f32[1,3,16,2048]{3,2,1,0:T(8,128)} copy(f32[1,3,16,2048]{3,2,1,0:T(8,128)} %bitcast.2) | data formatting | bytes 786432

commit v3 on v2

--- a/solution.py
+++ b/solution.py
@@ -15,9 +15,9 @@
 COARSE_STEP = 0.045
 LANES = 128
 SUB = 8
-HALO = 3
+HALO = (2, 2, 3)
 MESH = pl.DeviceIdType.MESH
-HIGHEST = lax.Precision.HIGHEST
+HIGH = lax.Precision.HIGH
 
 
 def line_tables(tiles, fine_tiles, stride, length, spacing, step):
@@ -133,7 +133,7 @@
     met = jnp.dot(
         jnp.concatenate([edge, total], axis=1),
         weights[...],
-        precision=HIGHEST,
+        precision=HIGH,
         preferred_element_type=jnp.float32,
     )
     value = met[:, :LANES]
@@ -152,8 +152,8 @@
 
 def kernel(
     tile_count, slices, x_hbm, fine_rows_hbm, fine_weights_hbm, coarse_rows_hbm,
-    coarse_weights_hbm, out_ref,
-    x_ref, fine_rows, fine_weights, coarse_rows, coarse_weights,
+    coarse_weights_hbm, fine_hbm, gain_ref,
+    natural, x_ref, fine_rows, fine_weights, coarse_rows, coarse_weights,
     up_main, down_main, edge, up_edge, down_edge, state, height, held,
     c_state, c_height, c_held, start, end, arrived, leaving, low, far_start, above_in, below_in,
     local, send, recv,
@@ -309,20 +309,53 @@
 
     lax.fori_loop(0, STEPS, fine_step, 0)
 
-    three = pl.ds(0, HALO)
-    part = (slice(None), slice(None), three)
+    last = planes - 1
+    first_part = (pl.ds(0, last), slice(None), pl.ds(0, HALO[0]))
+    last_part = (last, slice(None), pl.ds(0, HALO[last]))
     to_own = remote(leaving, arrived, 4, cut + 1, tile)
-    to_above = remote(leaving.at[part], below_in.at[part], 5, cut + 1, tile - 1)
-    to_below = remote(low.at[part], above_in.at[part], 6, cut + 1, tile + 1)
+    to_above = [
+        remote(leaving.at[part], below_in.at[part], 5 + i, cut + 1, tile - 1)
+        for i, part in enumerate((first_part, last_part))
+    ]
+    to_below = [
+        remote(low.at[part], above_in.at[part], 7 + i, cut + 1, tile + 1)
+        for i, part in enumerate((first_part, last_part))
+    ]
 
     def leave(plane, j, value):
         leaving[plane, j] = value
-        low[plane, j] = pltpu.roll(value, HALO, 0)
+        low[plane, j] = pltpu.roll(value, HALO[plane], 0)
+
+    def launch():
+        @pl.when(has_after & has_up)
+        def _():
+            for copy in to_above:
+                copy.start()
+
+        @pl.when(has_after & has_down)
+        def _():
+            for copy in to_below:
+                copy.start()
+
+        @pl.when(has_after)
+        def _():
+            to_own.start()
 
     @pl.when(cut == 0)
     def _():
         for plane, j in each_slab():
             leave(plane, j, restricted(plane, j, SUB, coarse_count))
+        launch()
+        gain_ref[...] = jnp.zeros_like(gain_ref)
+
+    for plane in range(planes):
+        for group in range(groups):
+            rows = pl.ds(SUB * (group + 1), SUB)
+            parts = relaid([state[plane, j, rows, :] for j in range(tiles)])
+            for t in range(tiles):
+                natural[plane, pl.ds(group * SUB, SUB), pl.ds(t * LANES, LANES)] = parts[t]
+    store = pltpu.make_async_copy(natural, fine_hbm, local.at[5])
+    store.start()
 
     @pl.when(has_before)
     def _():
@@ -339,19 +372,23 @@
 
         @pl.when(has_up)
         def _():
-            to_below.wait_recv()
+            for copy in to_below:
+                copy.wait_recv()
 
         @pl.when(has_down)
         def _():
-            to_above.wait_recv()
+            for copy in to_above:
+                copy.wait_recv()
 
         at = lax.broadcasted_iota(jnp.int32, (SUB, LANES), 0)
         for plane, j in each_slab():
             around = jnp.where(
-                at < HALO,
+                at < HALO[plane],
                 below_in[plane, j],
                 jnp.where(
-                    at >= SUB - HALO, pltpu.roll(above_in[plane, j], SUB - HALO, 0), 0.0
+                    at >= SUB - HALO[plane],
+                    pltpu.roll(above_in[plane, j], SUB - HALO[plane], 0),
+                    0.0,
                 ),
             )
             c_state[plane, j, pl.ds(coarse_count, SUB), :] = around - far_start[plane, j]
@@ -365,34 +402,11 @@
         )
         for plane, j in each_slab():
             leave(plane, j, c_state[plane, j, pl.ds(0, coarse_count), :] + end[plane, j])
-
-    @pl.when(has_after & has_up)
-    def _():
-        to_above.start()
-
-    @pl.when(has_after & has_down)
-    def _():
-        to_below.start()
-
-    @pl.when(has_after)
-    def _():
-        to_own.start()
-
-    @pl.when(has_before)
-    def _():
-        for plane in range(planes):
-            for j in range(tiles):
-                gain = c_state[plane, j // 2, pl.ds(0, coarse_count), :]
-                for r in range(2):
-                    at = pl.ds(SUB + r, coarse_count, stride=2)
-                    state[plane, j, at, :] = state[plane, j, at, :] + gain
-
-    for plane in range(planes):
-        for group in range(groups):
-            rows = pl.ds(SUB * (group + 1), SUB)
-            parts = relaid([state[plane, j, rows, :] for j in range(tiles)])
-            for t in range(tiles):
-                out_ref[plane, pl.ds(group * SUB, SUB), pl.ds(t * LANES, LANES)] = parts[t]
+        launch()
+        for plane, j in each_slab():
+            gain_ref[plane, j] = c_state[plane, j, pl.ds(0, coarse_count), :]
+
+    store.wait()
 
     @pl.when(has_down)
     def _():
@@ -406,15 +420,36 @@
 
     @pl.when(has_after & has_up)
     def _():
-        to_above.wait_send()
+        for copy in to_above:
+            copy.wait_send()
 
     @pl.when(has_after & has_down)
     def _():
-        to_below.wait_send()
+        for copy in to_below:
+            copy.wait_send()
 
     @pl.when(has_after)
     def _():
         to_own.wait_send()
+
+
+def finish(fine_ref, gain_ref, out_hbm, spread, result, done):
+    planes, tiles, row_count, _ = spread.shape
+    stores = []
+    for plane in range(planes):
+        parts = relaid([gain_ref[plane, j // 2] for j in range(tiles)])
+        for t in range(tiles):
+            for r in range(2):
+                spread[plane, t, pl.ds(r, row_count // 2, stride=2), :] = parts[t]
+        for t in range(tiles):
+            columns = pl.ds(t * LANES, LANES)
+            result[plane, :, columns] = fine_ref[plane, :, columns] + spread[plane, t]
+        stores.append(
+            pltpu.make_async_copy(result.at[plane], out_hbm.at[plane], done.at[plane])
+        )
+        stores[-1].start()
+    for store in stores:
+        store.wait()
 
 
 def per_device(tile_count, slices, start_states):
@@ -428,12 +463,18 @@
     coarse_count = row_count // 2
     f32 = jnp.float32
     slab = pltpu.VMEM((planes, half, coarse_count, LANES), f32)
-    out = pl.pallas_call(
+    fine_end, gain = pl.pallas_call(
         functools.partial(kernel, tile_count, slices),
-        out_shape=jax.ShapeDtypeStruct(fields.shape, f32),
+        out_shape=[
+            jax.ShapeDtypeStruct(fields.shape, f32),
+            jax.ShapeDtypeStruct((planes, half, coarse_count, LANES), f32),
+        ],
         in_specs=[pl.BlockSpec(memory_space=pl.ANY)] * 5,
-        out_specs=pl.BlockSpec(memory_space=pltpu.VMEM),
-        scratch_shapes=[pltpu.VMEM(fields.shape, f32)]
+        out_specs=[
+            pl.BlockSpec(memory_space=pl.ANY),
+            pl.BlockSpec(memory_space=pltpu.VMEM),
+        ],
+        scratch_shapes=[pltpu.VMEM(fields.shape, f32)] * 2
         + [pltpu.VMEM(a.shape, f32) for a in fine + coarse]
         + [pltpu.VMEM((planes, SUB, columns), f32)] * 2
         + [pltpu.VMEM((SUB, columns), f32)] * 3
@@ -447,12 +488,23 @@
         ]
         + [slab] * 8
         + [
-            pltpu.SemaphoreType.DMA((5,)),
-            pltpu.SemaphoreType.DMA((7,)),
-            pltpu.SemaphoreType.DMA((7,)),
+            pltpu.SemaphoreType.DMA((6,)),
+            pltpu.SemaphoreType.DMA((9,)),
+            pltpu.SemaphoreType.DMA((9,)),
         ],
         compiler_params=pltpu.CompilerParams(collective_id=0, has_side_effects=True),
     )(fields, *[jnp.asarray(a) for a in fine + coarse])
+    out = pl.pallas_call(
+        finish,
+        out_shape=jax.ShapeDtypeStruct(fields.shape, f32),
+        in_specs=[pl.BlockSpec(memory_space=pltpu.VMEM)] * 2,
+        out_specs=pl.BlockSpec(memory_space=pl.ANY),
+        scratch_shapes=[
+            pltpu.VMEM((planes, tiles, row_count, LANES), f32),
+            pltpu.VMEM(fields.shape, f32),
+            pltpu.SemaphoreType.DMA((planes,)),
+        ],
+    )(fine_end, gain)
     return out[None]
 
 

time: 31 us -> 29.2 us (0.942)
  local copies, waits for them, and re-layouts: 1.77 us -> 0 us
    unnamed x1 -> x0, local copies, waits for them, and re-layouts: 1.77 us -> none
    pallas_call x1 -> x2, Pallas kernels: 29 us -> 29 us  [the longest x1 26.9 us: per_device(): pl.pallas_call(functools.partial(kernel, tile_count, slices), out_shape=[...]
where the time goes in v3:
time: 29.2 us; the launch traced here: 29 us
  Pallas kernels  29 us (99%)
    pallas_call x1, Pallas kernels, per_device(): pl.pallas_call(functools.partial(kernel, tile_count, slices), out_shape=[...  26.9 us
    pallas_call x1, Pallas kernels, per_device(): pl.pallas_call(finish, out_shape=jax.ShapeDtypeStruct(fields.shape, f32),...  2.1 us

profile of v3, /device:TPU:27, one launch (start us, length us, event | category | flops | bytes accessed | tf_op | source)
XLA Modules:
  0.0 29.0 jit_solution(12379519988279033997)
XLA Ops:
  0.0 26.9 %shard_map.55 = (f32[3,16,2048]{2,1,0:T(8,128)}, f32[3,8,8,128]{3,2,1,0:T(8,128)}) custom-call(f32[3,16,2048]{2,1,0:T(8,128)} %bitcast.2, f32[5,16,128]{2,1,0:T(8,128)} %constant.8.clone.fine_rows_hbm, f32[256,256]{1,0:T(8,128)} %constant.9.clone.fine_weights_hbm, f32[5,8,128]{2,1,0:T(8,128)} %constant.10.clone.coarse_rows_hbm, ...), custom_call_target="tpu_custom_call" | custom-call | tf_op jit(solution)/shard_map/pallas_call | solution.py:466
  26.9 2.1 %shard_map.56 = f32[3,16,2048]{2,1,0:T(8,128)} custom-call(f32[3,16,2048]{2,1,0:T(8,128)} %get-tuple-element.7.fine_ref, f32[3,8,8,128]{3,2,1,0:T(8,128)} %get-tuple-element.8.gain_ref), custom_call_target="tpu_custom_call" | custom-call | tf_op jit(solution)/shard_map/pallas_call | solution.py:497
